TPU v7x, 256 devices: a whole 4x4x8 slice. The times are simulated.
256 devices in a mesh: section: 8 (over z), seq: 32 (over y, x, core).
Axes of the slice: x: 4, y: 4, z: 8, core: 2. Of those that a mesh axis runs over, the one named last changes fastest.
Arguments:
- stream_in: bfloat16 [2, 4096, 4096], P(None, 'seq'), may hold values from -30 to 30
- norm_gain: float32 [8, 4096], P('section'), may hold values from 0.25 to 1.75
- proj_weight: bfloat16 [8, 32, 4, 128, 128], P('section'), may hold values from -0.5 to 0.5
Outputs:
- streams: bfloat16 [8, 2, 4096, 4096], P('section', None, 'seq')
All inputs are finite; a program needn't handle non-finite values.
Results may differ from a plain program's by a relative error of at most 0.014.
Values may be sent and summed in bfloat16 or wider, within the bound.
No kernel may reach another device: no remote copies, remote signals or barrier semaphores. Data moves between devices by JAX's collectives and lax.ppermute only.
A program may use at most 64 MiB of HBM per device.

v0:
```python
import jax
import jax.numpy as jnp
from jax import lax
from jax.sharding import PartitionSpec as P

epsilon = 1e-05


def from_behind(x, axis, by):
    size = lax.axis_size(axis)
    pairs = [(i, i + by) for i in range(size) if 0 <= i + by < size]
    return lax.ppermute(x, axis, pairs)


def rms_scale(values):
    return lax.rsqrt(jnp.mean(values * values, axis=-1, keepdims=True) + epsilon)


def attend_block(query, key_part, value_part, carried_low):
    tok_rows = query.shape[0]
    inter = jnp.einsum("thc,hcd->thd", query, carried_low, preferred_element_type=jnp.float32)
    scores = jnp.einsum("thc,shc->hts", query, key_part, preferred_element_type=jnp.float32)
    causal = lax.broadcasted_iota(jnp.int32, (tok_rows, tok_rows), 0) >= lax.broadcasted_iota(
        jnp.int32, (tok_rows, tok_rows), 1
    )
    scores = jnp.where(causal[None], scores, jnp.zeros_like(scores)).astype(jnp.bfloat16)
    intra = jnp.einsum("hts,shd->thd", scores, value_part, preferred_element_type=jnp.float32)
    attn = inter + intra
    return (attn * rms_scale(attn)).astype(jnp.bfloat16)


def attend_blocks(query, key_part, value_part):
    states = jnp.einsum("bthc,bthd->bhcd", key_part, value_part, preferred_element_type=jnp.float32)
    running = jnp.cumsum(states, axis=0)
    carried = jnp.concatenate([jnp.zeros_like(states[:1]), running[:-1]], axis=0)
    return jax.vmap(attend_block)(query, key_part, value_part, carried.astype(jnp.bfloat16))


def project_heads(split, weights):
    mixed = jnp.einsum("thc,hjcd->jthd", split, weights[:, :3], preferred_element_type=jnp.float32)
    return jnp.concatenate([jax.nn.silu(mixed[:2]), mixed[2:]], axis=0).astype(jnp.bfloat16)


def apply_layer(stream, gain, weights):
    tok_rows, width = stream.shape
    head_count, head_size = (weights.shape[0], weights.shape[2])
    wide = stream.astype(jnp.float32)
    normed = (wide * rms_scale(wide) * gain).astype(jnp.bfloat16)
    parts = lax.axis_size("seq")
    group = head_count // parts
    grouped_in = normed.reshape(tok_rows, parts, group * head_size)
    received = lax.all_to_all(grouped_in, "seq", split_axis=1, concat_axis=0, tiled=True)
    owned = lax.dynamic_slice_in_dim(weights, lax.axis_index("seq") * group, group, 0)
    stacked = project_heads(received, owned)
    blocked = stacked.reshape(3, parts, tok_rows, group, head_size)
    local_out = attend_blocks(blocked[0], blocked[1], blocked[2])
    returned = lax.all_to_all(local_out, "seq", split_axis=0, concat_axis=2, tiled=True)
    head_out = returned.reshape(tok_rows, head_count, head_size)
    projected = jnp.einsum(
        "thc,hcd->thd", head_out, weights[:, 3], preferred_element_type=jnp.float32
    )
    return (wide + projected.reshape(tok_rows, width)).astype(jnp.bfloat16)


def on_device(stream_in, norm_gain, proj_weight):
    micro_count, tok_rows, width = stream_in.shape
    section_count = lax.axis_size("section")
    position = lax.axis_index("section")
    gain = norm_gain[0]
    weights = proj_weight[0]
    tick_count = micro_count + section_count - 1

    def one_tick(step_index, carry):
        incoming, saved = carry
        first_input = lax.dynamic_index_in_dim(
            stream_in, jnp.clip(step_index, 0, micro_count - 1).astype(jnp.int32), 0, keepdims=False
        )
        current = jnp.where(position == 0, first_input, incoming)
        result = apply_layer(current, gain, weights)
        slot_index = step_index - position
        valid = jnp.logical_and(slot_index >= 0, slot_index < micro_count)
        target = jnp.clip(slot_index, 0, micro_count - 1)
        previous = lax.dynamic_index_in_dim(saved, target, 0, keepdims=False)
        chosen = jnp.where(valid, result, previous)
        saved = lax.dynamic_update_index_in_dim(saved, chosen, target, 0)
        passed = from_behind(result, "section", 1)
        return (passed, saved)

    initial = (
        jnp.zeros((tok_rows, width), jnp.bfloat16),
        jnp.zeros((micro_count, tok_rows, width), jnp.bfloat16),
    )
    final_carry = lax.fori_loop(0, tick_count, one_tick, initial)
    return final_carry[1][None]


def solution(mesh):
    in_specs = (P(None, "seq", None), P("section", None), P("section", None, None, None, None))
    out_specs = P("section", None, "seq", None)
    return jax.shard_map(
        on_device, mesh=mesh, in_specs=in_specs, out_specs=out_specs, check_vma=False
    )
```

profile of v0, /device:TPU:128, one launch (start us, length us, event | category | flops | bytes accessed | tf_op | source)
XLA Modules:
  0.0 941.7 jit_solution(10498622832662492168)
XLA Ops:
  0.0 6.5 copy.26
  8.2 933.5 %while.16 = (s32[]{:T(128)}, bf16[128,4096]{0,1:T(8,128)(2,1)S(1)}, bf16[2,128,4096]{2,1,0:T(8,128)(2,1)}, pred[]{:T(512)}, bf16[2,128,4096]{2,1,0:T(8,128)(2,1)...) while((s32[]{:T(128)}, bf16[128,4096]{0,1:T(8,128)(2,1)S(1)}, ...), condition=%wide.region_4.5_spmd, body=%wide.region_0.4_spmd.sunk | while | flops 1105219712 | bytes 95472000 | solution.py:93
  12.8 7.3 all-to-all-start
  20.2 17.2 %all-to-all-done = bf16[128,32,128]{2,0,1:T(8,128)(2,1)S(1)} async-done(((bf16[128,32,128]{2,0,1:T(8,128)(2,1)}), bf16[128,32,128]{2,0,1:T(8,128)(2,1)S(1)}, u32[]{:S(2)}, u32[]{:S(2)}) %all-to-all-start) | async-done | bytes 1048608 | tf_op jit(solution)/shard_map/while/body/eval_jaxpr/all_to_all | solution.py:52
  52.5 4.8 fusion.70
  68.0 13.3 %all-to-all-done.1 = bf16[32,128,1,128]{1,3,2,0:T(8,128)(2,1)S(1)} async-done(((bf16[32,128,1,128]{1,3,2,0:T(8,128)(2,1)}), bf16[32,128,1,128]{1,3,2,0:T(8,128)(2,1)S(1)}, u32[]{:S(2)}, u32[]{:S(2)}) %all-to-all-start.1) | async-done | bytes 1048608 | tf_op jit(solution)/shard_map/while/body/eval_jaxpr/all_to_all | solution.py:57
  91.0 23.9 %collective-permute-done = bf16[128,4096]{0,1:T(8,128)(2,1)S(1)} collective-permute-done((bf16[128,4096]{0,1:T(8,128)(2,1)}, bf16[128,4096]{0,1:T(8,128)(2,1)S(1)}, u32[]{:S(2)}, u32[]{:S(2)}) %collective-permute-start) | collective-permute-done | bytes 1048608 | tf_op jit(solution)/shard_map/while/body/eval_jaxpr/ppermute | solution.py:12
  123.5 17.2 %all-to-all-done = bf16[128,32,128]{2,0,1:T(8,128)(2,1)S(1)} async-done(((bf16[128,32,128]{2,0,1:T(8,128)(2,1)}), bf16[128,32,128]{2,0,1:T(8,128)(2,1)S(1)}, u32[]{:S(2)}, u32[]{:S(2)}) %all-to-all-start) | async-done | bytes 1048608 | tf_op jit(solution)/shard_map/while/body/eval_jaxpr/all_to_all | solution.py:52
  171.4 13.3 %all-to-all-done.1 = bf16[32,128,1,128]{1,3,2,0:T(8,128)(2,1)S(1)} async-done(((bf16[32,128,1,128]{1,3,2,0:T(8,128)(2,1)}), bf16[32,128,1,128]{1,3,2,0:T(8,128)(2,1)S(1)}, u32[]{:S(2)}, u32[]{:S(2)}) %all-to-all-start.1) | async-done | bytes 1048608 | tf_op jit(solution)/shard_map/while/body/eval_jaxpr/all_to_all | solution.py:57
  193.3 25.0 %collective-permute-done = bf16[128,4096]{0,1:T(8,128)(2,1)S(1)} collective-permute-done((bf16[128,4096]{0,1:T(8,128)(2,1)}, bf16[128,4096]{0,1:T(8,128)(2,1)S(1)}, u32[]{:S(2)}, u32[]{:S(2)}) %collective-permute-start) | collective-permute-done | bytes 1048608 | tf_op jit(solution)/shard_map/while/body/eval_jaxpr/ppermute | solution.py:12
  226.9 17.2 %all-to-all-done = bf16[128,32,128]{2,0,1:T(8,128)(2,1)S(1)} async-done(((bf16[128,32,128]{2,0,1:T(8,128)(2,1)}), bf16[128,32,128]{2,0,1:T(8,128)(2,1)S(1)}, u32[]{:S(2)}, u32[]{:S(2)}) %all-to-all-start) | async-done | bytes 1048608 | tf_op jit(solution)/shard_map/while/body/eval_jaxpr/all_to_all | solution.py:52
  274.7 13.3 %all-to-all-done.1 = bf16[32,128,1,128]{1,3,2,0:T(8,128)(2,1)S(1)} async-done(((bf16[32,128,1,128]{1,3,2,0:T(8,128)(2,1)}), bf16[32,128,1,128]{1,3,2,0:T(8,128)(2,1)S(1)}, u32[]{:S(2)}, u32[]{:S(2)}) %all-to-all-start.1) | async-done | bytes 1048608 | tf_op jit(solution)/shard_map/while/body/eval_jaxpr/all_to_all | solution.py:57
  296.7 25.0 %collective-permute-done = bf16[128,4096]{0,1:T(8,128)(2,1)S(1)} collective-permute-done((bf16[128,4096]{0,1:T(8,128)(2,1)}, bf16[128,4096]{0,1:T(8,128)(2,1)S(1)}, u32[]{:S(2)}, u32[]{:S(2)}) %collective-permute-start) | collective-permute-done | bytes 1048608 | tf_op jit(solution)/shard_map/while/body/eval_jaxpr/ppermute | solution.py:12
  330.2 17.2 %all-to-all-done = bf16[128,32,128]{2,0,1:T(8,128)(2,1)S(1)} async-done(((bf16[128,32,128]{2,0,1:T(8,128)(2,1)}), bf16[128,32,128]{2,0,1:T(8,128)(2,1)S(1)}, u32[]{:S(2)}, u32[]{:S(2)}) %all-to-all-start) | async-done | bytes 1048608 | tf_op jit(solution)/shard_map/while/body/eval_jaxpr/all_to_all | solution.py:52
  378.0 13.3 %all-to-all-done.1 = bf16[32,128,1,128]{1,3,2,0:T(8,128)(2,1)S(1)} async-done(((bf16[32,128,1,128]{1,3,2,0:T(8,128)(2,1)}), bf16[32,128,1,128]{1,3,2,0:T(8,128)(2,1)S(1)}, u32[]{:S(2)}, u32[]{:S(2)}) %all-to-all-start.1) | async-done | bytes 1048608 | tf_op jit(solution)/shard_map/while/body/eval_jaxpr/all_to_all | solution.py:57
  400.0 25.0 %collective-permute-done = bf16[128,4096]{0,1:T(8,128)(2,1)S(1)} collective-permute-done((bf16[128,4096]{0,1:T(8,128)(2,1)}, bf16[128,4096]{0,1:T(8,128)(2,1)S(1)}, u32[]{:S(2)}, u32[]{:S(2)}) %collective-permute-start) | collective-permute-done | bytes 1048608 | tf_op jit(solution)/shard_map/while/body/eval_jaxpr/ppermute | solution.py:12
  433.6 17.2 %all-to-all-done = bf16[128,32,128]{2,0,1:T(8,128)(2,1)S(1)} async-done(((bf16[128,32,128]{2,0,1:T(8,128)(2,1)}), bf16[128,32,128]{2,0,1:T(8,128)(2,1)S(1)}, u32[]{:S(2)}, u32[]{:S(2)}) %all-to-all-start) | async-done | bytes 1048608 | tf_op jit(solution)/shard_map/while/body/eval_jaxpr/all_to_all | solution.py:52
  481.4 13.3 %all-to-all-done.1 = bf16[32,128,1,128]{1,3,2,0:T(8,128)(2,1)S(1)} async-done(((bf16[32,128,1,128]{1,3,2,0:T(8,128)(2,1)}), bf16[32,128,1,128]{1,3,2,0:T(8,128)(2,1)S(1)}, u32[]{:S(2)}, u32[]{:S(2)}) %all-to-all-start.1) | async-done | bytes 1048608 | tf_op jit(solution)/shard_map/while/body/eval_jaxpr/all_to_all | solution.py:57
  503.4 25.0 %collective-permute-done = bf16[128,4096]{0,1:T(8,128)(2,1)S(1)} collective-permute-done((bf16[128,4096]{0,1:T(8,128)(2,1)}, bf16[128,4096]{0,1:T(8,128)(2,1)S(1)}, u32[]{:S(2)}, u32[]{:S(2)}) %collective-permute-start) | collective-permute-done | bytes 1048608 | tf_op jit(solution)/shard_map/while/body/eval_jaxpr/ppermute | solution.py:12
  536.9 17.2 %all-to-all-done = bf16[128,32,128]{2,0,1:T(8,128)(2,1)S(1)} async-done(((bf16[128,32,128]{2,0,1:T(8,128)(2,1)}), bf16[128,32,128]{2,0,1:T(8,128)(2,1)S(1)}, u32[]{:S(2)}, u32[]{:S(2)}) %all-to-all-start) | async-done | bytes 1048608 | tf_op jit(solution)/shard_map/while/body/eval_jaxpr/all_to_all | solution.py:52
  584.7 13.3 %all-to-all-done.1 = bf16[32,128,1,128]{1,3,2,0:T(8,128)(2,1)S(1)} async-done(((bf16[32,128,1,128]{1,3,2,0:T(8,128)(2,1)}), bf16[32,128,1,128]{1,3,2,0:T(8,128)(2,1)S(1)}, u32[]{:S(2)}, u32[]{:S(2)}) %all-to-all-start.1) | async-done | bytes 1048608 | tf_op jit(solution)/shard_map/while/body/eval_jaxpr/all_to_all | solution.py:57
  606.7 25.0 %collective-permute-done = bf16[128,4096]{0,1:T(8,128)(2,1)S(1)} collective-permute-done((bf16[128,4096]{0,1:T(8,128)(2,1)}, bf16[128,4096]{0,1:T(8,128)(2,1)S(1)}, u32[]{:S(2)}, u32[]{:S(2)}) %collective-permute-start) | collective-permute-done | bytes 1048608 | tf_op jit(solution)/shard_map/while/body/eval_jaxpr/ppermute | solution.py:12
  640.2 17.2 %all-to-all-done = bf16[128,32,128]{2,0,1:T(8,128)(2,1)S(1)} async-done(((bf16[128,32,128]{2,0,1:T(8,128)(2,1)}), bf16[128,32,128]{2,0,1:T(8,128)(2,1)S(1)}, u32[]{:S(2)}, u32[]{:S(2)}) %all-to-all-start) | async-done | bytes 1048608 | tf_op jit(solution)/shard_map/while/body/eval_jaxpr/all_to_all | solution.py:52
  688.1 13.3 %all-to-all-done.1 = bf16[32,128,1,128]{1,3,2,0:T(8,128)(2,1)S(1)} async-done(((bf16[32,128,1,128]{1,3,2,0:T(8,128)(2,1)}), bf16[32,128,1,128]{1,3,2,0:T(8,128)(2,1)S(1)}, u32[]{:S(2)}, u32[]{:S(2)}) %all-to-all-start.1) | async-done | bytes 1048608 | tf_op jit(solution)/shard_map/while/body/eval_jaxpr/all_to_all | solution.py:57
  710.0 25.0 %collective-permute-done = bf16[128,4096]{0,1:T(8,128)(2,1)S(1)} collective-permute-done((bf16[128,4096]{0,1:T(8,128)(2,1)}, bf16[128,4096]{0,1:T(8,128)(2,1)S(1)}, u32[]{:S(2)}, u32[]{:S(2)}) %collective-permute-start) | collective-permute-done | bytes 1048608 | tf_op jit(solution)/shard_map/while/body/eval_jaxpr/ppermute | solution.py:12
  743.6 17.2 %all-to-all-done = bf16[128,32,128]{2,0,1:T(8,128)(2,1)S(1)} async-done(((bf16[128,32,128]{2,0,1:T(8,128)(2,1)}), bf16[128,32,128]{2,0,1:T(8,128)(2,1)S(1)}, u32[]{:S(2)}, u32[]{:S(2)}) %all-to-all-start) | async-done | bytes 1048608 | tf_op jit(solution)/shard_map/while/body/eval_jaxpr/all_to_all | solution.py:52
  775.9 4.8 fusion.70
  791.4 13.3 %all-to-all-done.1 = bf16[32,128,1,128]{1,3,2,0:T(8,128)(2,1)S(1)} async-done(((bf16[32,128,1,128]{1,3,2,0:T(8,128)(2,1)}), bf16[32,128,1,128]{1,3,2,0:T(8,128)(2,1)S(1)}, u32[]{:S(2)}, u32[]{:S(2)}) %all-to-all-start.1) | async-done | bytes 1048608 | tf_op jit(solution)/shard_map/while/body/eval_jaxpr/all_to_all | solution.py:57
  813.4 25.0 %collective-permute-done = bf16[128,4096]{0,1:T(8,128)(2,1)S(1)} collective-permute-done((bf16[128,4096]{0,1:T(8,128)(2,1)}, bf16[128,4096]{0,1:T(8,128)(2,1)S(1)}, u32[]{:S(2)}, u32[]{:S(2)}) %collective-permute-start) | collective-permute-done | bytes 1048608 | tf_op jit(solution)/shard_map/while/body/eval_jaxpr/ppermute | solution.py:12
  846.9 17.2 %all-to-all-done = bf16[128,32,128]{2,0,1:T(8,128)(2,1)S(1)} async-done(((bf16[128,32,128]{2,0,1:T(8,128)(2,1)}), bf16[128,32,128]{2,0,1:T(8,128)(2,1)S(1)}, u32[]{:S(2)}, u32[]{:S(2)}) %all-to-all-start) | async-done | bytes 1048608 | tf_op jit(solution)/shard_map/while/body/eval_jaxpr/all_to_all | solution.py:52
  894.8 13.3 %all-to-all-done.1 = bf16[32,128,1,128]{1,3,2,0:T(8,128)(2,1)S(1)} async-done(((bf16[32,128,1,128]{1,3,2,0:T(8,128)(2,1)}), bf16[32,128,1,128]{1,3,2,0:T(8,128)(2,1)S(1)}, u32[]{:S(2)}, u32[]{:S(2)}) %all-to-all-start.1) | async-done | bytes 1048608 | tf_op jit(solution)/shard_map/while/body/eval_jaxpr/all_to_all | solution.py:57
  916.7 25.0 %collective-permute-done = bf16[128,4096]{0,1:T(8,128)(2,1)S(1)} collective-permute-done((bf16[128,4096]{0,1:T(8,128)(2,1)}, bf16[128,4096]{0,1:T(8,128)(2,1)S(1)}, u32[]{:S(2)}, u32[]{:S(2)}) %collective-permute-start) | collective-permute-done | bytes 1048608 | tf_op jit(solution)/shard_map/while/body/eval_jaxpr/ppermute | solution.py:12
  (289 shorter events, 419.3 us)
Async XLA Ops:
  6.5 1.7 copy-start
  12.8 24.5 %all-to-all-start = ((bf16[128,32,128]{2,0,1:T(8,128)(2,1)}), bf16[128,32,128]{2,0,1:T(8,128)(2,1)S(1)}, u32[]{:S(2)}, u32[]{:S(2)}) async-start(bf16[128,32,128]{2,0,1:T(8,128)(2,1)} %copy.74), calls=%async_computation | async-start | bytes 2097152 | tf_op jit(solution)/shard_map/while/body/eval_jaxpr/all_to_all | solution.py:52
  60.1 21.1 %all-to-all-start.1 = ((bf16[32,128,1,128]{1,3,2,0:T(8,128)(2,1)}), bf16[32,128,1,128]{1,3,2,0:T(8,128)(2,1)S(1)}, u32[]{:S(2)}, u32[]{:S(2)}) async-start(bf16[32,128,1,128]{1,3,2,0:T(8,128)(2,1)} %fusion.71), calls=%async_computation.1 | async-start | bytes 2097152 | tf_op jit(solution)/shard_map/while/body/eval_jaxpr/all_to_all | solution.py:57
  86.5 28.5 %collective-permute-start = (bf16[128,4096]{0,1:T(8,128)(2,1)}, bf16[128,4096]{0,1:T(8,128)(2,1)S(1)}, u32[]{:S(2)}, u32[]{:S(2)}) collective-permute-start(bf16[128,4096]{0,1:T(8,128)(2,1)} %get-tuple-element.266), channel_id=1, source_target_pairs={{0,32},{32,64},{64,96},{96,128},{128,160},{160,192},{192,224},{1,3... | collective-permute-start | bytes 3145736 | tf_op jit(solution)/shard_map/while/body/eval_jaxpr/ppermute | solution.py:12
  119.6 21.1 %all-to-all-start = ((bf16[128,32,128]{2,0,1:T(8,128)(2,1)}), bf16[128,32,128]{2,0,1:T(8,128)(2,1)S(1)}, u32[]{:S(2)}, u32[]{:S(2)}) async-start(bf16[128,32,128]{2,0,1:T(8,128)(2,1)} %copy.74), calls=%async_computation | async-start | bytes 2097152 | tf_op jit(solution)/shard_map/while/body/eval_jaxpr/all_to_all | solution.py:52
  163.5 21.1 %all-to-all-start.1 = ((bf16[32,128,1,128]{1,3,2,0:T(8,128)(2,1)}), bf16[32,128,1,128]{1,3,2,0:T(8,128)(2,1)S(1)}, u32[]{:S(2)}, u32[]{:S(2)}) async-start(bf16[32,128,1,128]{1,3,2,0:T(8,128)(2,1)} %fusion.71), calls=%async_computation.1 | async-start | bytes 2097152 | tf_op jit(solution)/shard_map/while/body/eval_jaxpr/all_to_all | solution.py:57
  189.8 28.5 %collective-permute-start = (bf16[128,4096]{0,1:T(8,128)(2,1)}, bf16[128,4096]{0,1:T(8,128)(2,1)S(1)}, u32[]{:S(2)}, u32[]{:S(2)}) collective-permute-start(bf16[128,4096]{0,1:T(8,128)(2,1)} %get-tuple-element.266), channel_id=1, source_target_pairs={{0,32},{32,64},{64,96},{96,128},{128,160},{160,192},{192,224},{1,3... | collective-permute-start | bytes 3145736 | tf_op jit(solution)/shard_map/while/body/eval_jaxpr/ppermute | solution.py:12
  222.9 21.1 %all-to-all-start = ((bf16[128,32,128]{2,0,1:T(8,128)(2,1)}), bf16[128,32,128]{2,0,1:T(8,128)(2,1)S(1)}, u32[]{:S(2)}, u32[]{:S(2)}) async-start(bf16[128,32,128]{2,0,1:T(8,128)(2,1)} %copy.74), calls=%async_computation | async-start | bytes 2097152 | tf_op jit(solution)/shard_map/while/body/eval_jaxpr/all_to_all | solution.py:52
  266.8 21.1 %all-to-all-start.1 = ((bf16[32,128,1,128]{1,3,2,0:T(8,128)(2,1)}), bf16[32,128,1,128]{1,3,2,0:T(8,128)(2,1)S(1)}, u32[]{:S(2)}, u32[]{:S(2)}) async-start(bf16[32,128,1,128]{1,3,2,0:T(8,128)(2,1)} %fusion.71), calls=%async_computation.1 | async-start | bytes 2097152 | tf_op jit(solution)/shard_map/while/body/eval_jaxpr/all_to_all | solution.py:57
  293.2 28.5 %collective-permute-start = (bf16[128,4096]{0,1:T(8,128)(2,1)}, bf16[128,4096]{0,1:T(8,128)(2,1)S(1)}, u32[]{:S(2)}, u32[]{:S(2)}) collective-permute-start(bf16[128,4096]{0,1:T(8,128)(2,1)} %get-tuple-element.266), channel_id=1, source_target_pairs={{0,32},{32,64},{64,96},{96,128},{128,160},{160,192},{192,224},{1,3... | collective-permute-start | bytes 3145736 | tf_op jit(solution)/shard_map/while/body/eval_jaxpr/ppermute | solution.py:12
  326.2 21.1 %all-to-all-start = ((bf16[128,32,128]{2,0,1:T(8,128)(2,1)}), bf16[128,32,128]{2,0,1:T(8,128)(2,1)S(1)}, u32[]{:S(2)}, u32[]{:S(2)}) async-start(bf16[128,32,128]{2,0,1:T(8,128)(2,1)} %copy.74), calls=%async_computation | async-start | bytes 2097152 | tf_op jit(solution)/shard_map/while/body/eval_jaxpr/all_to_all | solution.py:52
  370.2 21.1 %all-to-all-start.1 = ((bf16[32,128,1,128]{1,3,2,0:T(8,128)(2,1)}), bf16[32,128,1,128]{1,3,2,0:T(8,128)(2,1)S(1)}, u32[]{:S(2)}, u32[]{:S(2)}) async-start(bf16[32,128,1,128]{1,3,2,0:T(8,128)(2,1)} %fusion.71), calls=%async_computation.1 | async-start | bytes 2097152 | tf_op jit(solution)/shard_map/while/body/eval_jaxpr/all_to_all | solution.py:57
  396.5 28.5 %collective-permute-start = (bf16[128,4096]{0,1:T(8,128)(2,1)}, bf16[128,4096]{0,1:T(8,128)(2,1)S(1)}, u32[]{:S(2)}, u32[]{:S(2)}) collective-permute-start(bf16[128,4096]{0,1:T(8,128)(2,1)} %get-tuple-element.266), channel_id=1, source_target_pairs={{0,32},{32,64},{64,96},{96,128},{128,160},{160,192},{192,224},{1,3... | collective-permute-start | bytes 3145736 | tf_op jit(solution)/shard_map/while/body/eval_jaxpr/ppermute | solution.py:12
  429.6 21.1 %all-to-all-start = ((bf16[128,32,128]{2,0,1:T(8,128)(2,1)}), bf16[128,32,128]{2,0,1:T(8,128)(2,1)S(1)}, u32[]{:S(2)}, u32[]{:S(2)}) async-start(bf16[128,32,128]{2,0,1:T(8,128)(2,1)} %copy.74), calls=%async_computation | async-start | bytes 2097152 | tf_op jit(solution)/shard_map/while/body/eval_jaxpr/all_to_all | solution.py:52
  473.5 21.1 %all-to-all-start.1 = ((bf16[32,128,1,128]{1,3,2,0:T(8,128)(2,1)}), bf16[32,128,1,128]{1,3,2,0:T(8,128)(2,1)S(1)}, u32[]{:S(2)}, u32[]{:S(2)}) async-start(bf16[32,128,1,128]{1,3,2,0:T(8,128)(2,1)} %fusion.71), calls=%async_computation.1 | async-start | bytes 2097152 | tf_op jit(solution)/shard_map/while/body/eval_jaxpr/all_to_all | solution.py:57
  499.8 28.5 %collective-permute-start = (bf16[128,4096]{0,1:T(8,128)(2,1)}, bf16[128,4096]{0,1:T(8,128)(2,1)S(1)}, u32[]{:S(2)}, u32[]{:S(2)}) collective-permute-start(bf16[128,4096]{0,1:T(8,128)(2,1)} %get-tuple-element.266), channel_id=1, source_target_pairs={{0,32},{32,64},{64,96},{96,128},{128,160},{160,192},{192,224},{1,3... | collective-permute-start | bytes 3145736 | tf_op jit(solution)/shard_map/while/body/eval_jaxpr/ppermute | solution.py:12
  532.9 21.1 %all-to-all-start = ((bf16[128,32,128]{2,0,1:T(8,128)(2,1)}), bf16[128,32,128]{2,0,1:T(8,128)(2,1)S(1)}, u32[]{:S(2)}, u32[]{:S(2)}) async-start(bf16[128,32,128]{2,0,1:T(8,128)(2,1)} %copy.74), calls=%async_computation | async-start | bytes 2097152 | tf_op jit(solution)/shard_map/while/body/eval_jaxpr/all_to_all | solution.py:52
  576.9 21.1 %all-to-all-start.1 = ((bf16[32,128,1,128]{1,3,2,0:T(8,128)(2,1)}), bf16[32,128,1,128]{1,3,2,0:T(8,128)(2,1)S(1)}, u32[]{:S(2)}, u32[]{:S(2)}) async-start(bf16[32,128,1,128]{1,3,2,0:T(8,128)(2,1)} %fusion.71), calls=%async_computation.1 | async-start | bytes 2097152 | tf_op jit(solution)/shard_map/while/body/eval_jaxpr/all_to_all | solution.py:57
  603.2 28.5 %collective-permute-start = (bf16[128,4096]{0,1:T(8,128)(2,1)}, bf16[128,4096]{0,1:T(8,128)(2,1)S(1)}, u32[]{:S(2)}, u32[]{:S(2)}) collective-permute-start(bf16[128,4096]{0,1:T(8,128)(2,1)} %get-tuple-element.266), channel_id=1, source_target_pairs={{0,32},{32,64},{64,96},{96,128},{128,160},{160,192},{192,224},{1,3... | collective-permute-start | bytes 3145736 | tf_op jit(solution)/shard_map/while/body/eval_jaxpr/ppermute | solution.py:12
  636.3 21.1 %all-to-all-start = ((bf16[128,32,128]{2,0,1:T(8,128)(2,1)}), bf16[128,32,128]{2,0,1:T(8,128)(2,1)S(1)}, u32[]{:S(2)}, u32[]{:S(2)}) async-start(bf16[128,32,128]{2,0,1:T(8,128)(2,1)} %copy.74), calls=%async_computation | async-start | bytes 2097152 | tf_op jit(solution)/shard_map/while/body/eval_jaxpr/all_to_all | solution.py:52
  680.2 21.1 %all-to-all-start.1 = ((bf16[32,128,1,128]{1,3,2,0:T(8,128)(2,1)}), bf16[32,128,1,128]{1,3,2,0:T(8,128)(2,1)S(1)}, u32[]{:S(2)}, u32[]{:S(2)}) async-start(bf16[32,128,1,128]{1,3,2,0:T(8,128)(2,1)} %fusion.71), calls=%async_computation.1 | async-start | bytes 2097152 | tf_op jit(solution)/shard_map/while/body/eval_jaxpr/all_to_all | solution.py:57
  706.5 28.5 %collective-permute-start = (bf16[128,4096]{0,1:T(8,128)(2,1)}, bf16[128,4096]{0,1:T(8,128)(2,1)S(1)}, u32[]{:S(2)}, u32[]{:S(2)}) collective-permute-start(bf16[128,4096]{0,1:T(8,128)(2,1)} %get-tuple-element.266), channel_id=1, source_target_pairs={{0,32},{32,64},{64,96},{96,128},{128,160},{160,192},{192,224},{1,3... | collective-permute-start | bytes 3145736 | tf_op jit(solution)/shard_map/while/body/eval_jaxpr/ppermute | solution.py:12
  739.6 21.1 %all-to-all-start = ((bf16[128,32,128]{2,0,1:T(8,128)(2,1)}), bf16[128,32,128]{2,0,1:T(8,128)(2,1)S(1)}, u32[]{:S(2)}, u32[]{:S(2)}) async-start(bf16[128,32,128]{2,0,1:T(8,128)(2,1)} %copy.74), calls=%async_computation | async-start | bytes 2097152 | tf_op jit(solution)/shard_map/while/body/eval_jaxpr/all_to_all | solution.py:52
  783.5 21.1 %all-to-all-start.1 = ((bf16[32,128,1,128]{1,3,2,0:T(8,128)(2,1)}), bf16[32,128,1,128]{1,3,2,0:T(8,128)(2,1)S(1)}, u32[]{:S(2)}, u32[]{:S(2)}) async-start(bf16[32,128,1,128]{1,3,2,0:T(8,128)(2,1)} %fusion.71), calls=%async_computation.1 | async-start | bytes 2097152 | tf_op jit(solution)/shard_map/while/body/eval_jaxpr/all_to_all | solution.py:57
  809.9 28.5 %collective-permute-start = (bf16[128,4096]{0,1:T(8,128)(2,1)}, bf16[128,4096]{0,1:T(8,128)(2,1)S(1)}, u32[]{:S(2)}, u32[]{:S(2)}) collective-permute-start(bf16[128,4096]{0,1:T(8,128)(2,1)} %get-tuple-element.266), channel_id=1, source_target_pairs={{0,32},{32,64},{64,96},{96,128},{128,160},{160,192},{192,224},{1,3... | collective-permute-start | bytes 3145736 | tf_op jit(solution)/shard_map/while/body/eval_jaxpr/ppermute | solution.py:12
  843.0 21.1 %all-to-all-start = ((bf16[128,32,128]{2,0,1:T(8,128)(2,1)}), bf16[128,32,128]{2,0,1:T(8,128)(2,1)S(1)}, u32[]{:S(2)}, u32[]{:S(2)}) async-start(bf16[128,32,128]{2,0,1:T(8,128)(2,1)} %copy.74), calls=%async_computation | async-start | bytes 2097152 | tf_op jit(solution)/shard_map/while/body/eval_jaxpr/all_to_all | solution.py:52
  886.9 21.1 %all-to-all-start.1 = ((bf16[32,128,1,128]{1,3,2,0:T(8,128)(2,1)}), bf16[32,128,1,128]{1,3,2,0:T(8,128)(2,1)S(1)}, u32[]{:S(2)}, u32[]{:S(2)}) async-start(bf16[32,128,1,128]{1,3,2,0:T(8,128)(2,1)} %fusion.71), calls=%async_computation.1 | async-start | bytes 2097152 | tf_op jit(solution)/shard_map/while/body/eval_jaxpr/all_to_all | solution.py:57
  913.2 28.5 %collective-permute-start = (bf16[128,4096]{0,1:T(8,128)(2,1)}, bf16[128,4096]{0,1:T(8,128)(2,1)S(1)}, u32[]{:S(2)}, u32[]{:S(2)}) collective-permute-start(bf16[128,4096]{0,1:T(8,128)(2,1)} %get-tuple-element.266), channel_id=1, source_target_pairs={{0,32},{32,64},{64,96},{96,128},{128,160},{160,192},{192,224},{1,3... | collective-permute-start | bytes 3145736 | tf_op jit(solution)/shard_map/while/body/eval_jaxpr/ppermute | solution.py:12
where the time goes:
time: 947 us; the launch traced here: 942 us
  waiting for transfers between devices  498 us (53%)
  local copies, waits for them, and re-layouts  167 us (18%)
  matrix products  121 us (13%)
  starting transfers between devices  92.3 us (10%)
  other arithmetic  62.3 us (7%)
    ppermute x9, waiting for transfers between devices, from_behind(): return lax.ppermute(x, axis, pairs)  224 us
    all_to_all x9, waiting for transfers between devices, apply_layer(): lax.all_to_all(grouped_in, 'seq', split_axis=1, concat_axis=0, tiled=True)  155 us
    all_to_all x9, waiting for transfers between devices, apply_layer(): lax.all_to_all(local_out, 'seq', split_axis=0, concat_axis=2, tiled=True)  119 us
    dot_general x9, matrix products, attend_block(): jnp.einsum('hts,shd->thd', scores, value_part, preferred_element_type=jnp...  42.9 us
    all_to_all x9, starting transfers between devices, apply_layer(): lax.all_to_all(grouped_in, 'seq', split_axis=1, concat_axis=0, tiled=True)  38.8 us
    while x45, local copies, waits for them, and re-layouts  36.7 us
    all_to_all x9, starting transfers between devices, apply_layer(): lax.all_to_all(local_out, 'seq', split_axis=0, concat_axis=2, tiled=True)  35.3 us
    dynamic_slice x18, local copies, waits for them, and re-layouts, one_tick(): previous = lax.dynamic_index_in_dim(saved, target, 0, keepdims=False)  35.2 us
  transfers between devices with their start and end apart: 27, of which 27 were waited for; matrix products, arithmetic and copies ran while one was open for 5% of the time, Pallas kernels for 0%

commit v1 on v0

--- a/solution.py
+++ b/solution.py
@@ -54,7 +54,10 @@
     stacked = project_heads(received, owned)
     blocked = stacked.reshape(3, parts, tok_rows, group, head_size)
     local_out = attend_blocks(blocked[0], blocked[1], blocked[2])
-    returned = lax.all_to_all(local_out, "seq", split_axis=0, concat_axis=2, tiled=True)
+    returned = jnp.concatenate(
+        lax.all_to_all(jnp.stack(jnp.split(local_out, lax.axis_size("seq"), axis=0)), "seq", 0, 0),
+        axis=2,
+    )
     head_out = returned.reshape(tok_rows, head_count, head_size)
     projected = jnp.einsum(
         "thc,hcd->thd", head_out, weights[:, 3], preferred_element_type=jnp.float32

time: 947 us -> 1100 us (1.16)
  local copies, waits for them, and re-layouts: 167 us -> 311 us
  waiting for transfers between devices: 498 us -> 515 us
    while x45 -> x324, local copies, waits for them, and re-layouts: 36.7 us -> 205 us
    dynamic_slice x18, local copies, waits for them, and re-layouts: 35.2 us -> 17.6 us  [one_tick(): previous = lax.dynamic_index_in_dim(saved, target, 0, keepdims=False)]
    all_to_all x9, waiting for transfers between devices: 119 us -> 137 us  [apply_layer(): lax.all_to_all(jnp.stack(jnp.split(local_out, lax.axis_size('seq'), axis=...]
    all_to_all x9 -> x0, local copies, waits for them, and re-layouts: 12 us -> none  [apply_layer(): lax.all_to_all(local_out, 'seq', split_axis=0, concat_axis=2, tiled=True)]
    another operation x9 -> x18, local copies, waits for them, and re-layouts: 20.4 us -> 25.9 us
  transfers between devices with their start and end apart: 27 -> 27, of which waited for: 27 -> 27; matrix products, arithmetic and copies ran while one was open for 5% -> 3% of each run, Pallas kernels for 0% -> 0%
where the time goes in v1:
time: 1100 us
  waiting for transfers between devices  515 us (47%)
  local copies, waits for them, and re-layouts  311 us (28%)
  matrix products  117 us (11%)
  starting transfers between devices  98.9 us (9%)
  other arithmetic  55.3 us (5%)
    ppermute x9, waiting for transfers between devices, from_behind(): return lax.ppermute(x, axis, pairs)  224 us
    while x324, local copies, waits for them, and re-layouts  205 us
    all_to_all x9, waiting for transfers between devices, apply_layer(): lax.all_to_all(grouped_in, 'seq', split_axis=1, concat_axis=0, tiled=True)  155 us
    all_to_all x9, waiting for transfers between devices, apply_layer(): lax.all_to_all(jnp.stack(jnp.split(local_out, lax.axis_size('seq'), axis=...  137 us
    dot_general x9, matrix products, attend_block(): jnp.einsum('hts,shd->thd', scores, value_part, preferred_element_type=jnp...  42.9 us
    all_to_all x9, starting transfers between devices, apply_layer(): lax.all_to_all(jnp.stack(jnp.split(local_out, lax.axis_size('seq'), axis=...  41.9 us
    all_to_all x9, starting transfers between devices, apply_layer(): lax.all_to_all(grouped_in, 'seq', split_axis=1, concat_axis=0, tiled=True)  38.8 us
    dot_general x9, matrix products, attend_block(): jnp.einsum('thc,hcd->thd', query, carried_low, preferred_element_type=jnp...  33.1 us
  transfers between devices with their start and end apart: 27, of which 27 were waited for; matrix products, arithmetic and copies ran while one was open for 3% of the time, Pallas kernels for 0%

profile of v1, /device:TPU:128, one launch (start us, length us, event | category | flops | bytes accessed | tf_op | source)
XLA Modules:
  0.0 1099.2 jit_solution(2733746130287784773)
XLA Ops:
  0.0 6.5 copy.44
  8.2 1091.1 %while.16 = (s32[]{:T(128)}, bf16[128,4096]{0,1:T(8,128)(2,1)S(1)}, bf16[2,128,4096]{2,1,0:T(8,128)(2,1)}, pred[]{:T(512)}, bf16[2,128,4096]{2,1,0:T(8,128)(2,1)...) while((s32[]{:T(128)}, bf16[128,4096]{0,1:T(8,128)(2,1)S(1)}, ...), condition=%wide.region_4.5_spmd, body=%wide.region_0.4_spmd.sunk | while | flops 1105219712 | bytes 96520576 | solution.py:96
  12.8 7.3 all-to-all-start
  20.1 17.2 %all-to-all-done = bf16[128,32,128]{2,0,1:T(8,128)(2,1)S(1)} async-done(((bf16[128,32,128]{2,0,1:T(8,128)(2,1)}), bf16[128,32,128]{2,0,1:T(8,128)(2,1)S(1)}, u32[]{:S(2)}, u32[]{:S(2)}) %all-to-all-start) | async-done | bytes 1048608 | tf_op jit(solution)/shard_map/while/body/eval_jaxpr/all_to_all | solution.py:52
  52.4 4.8 fusion.71
  85.3 15.2 %all-to-all-done.1 = bf16[32,1,128,1,128]{2,4,3,1,0:T(8,128)(2,1)} async-done(((bf16[32,1,128,1,128]{2,4,3,1,0:T(8,128)(2,1)}), bf16[32,1,128,1,128]{2,4,3,1,0:T(8,128)(2,1)}, u32[]{:S(2)}, u32[]{:S(2)}) %all-to-all-start.1) | async-done | bytes 1048608 | tf_op jit(solution)/shard_map/while/body/eval_jaxpr/all_to_all | solution.py:58
  108.5 24.0 %collective-permute-done = bf16[128,4096]{0,1:T(8,128)(2,1)S(1)} collective-permute-done((bf16[128,4096]{0,1:T(8,128)(2,1)}, bf16[128,4096]{0,1:T(8,128)(2,1)S(1)}, u32[]{:S(2)}, u32[]{:S(2)}) %collective-permute-start) | collective-permute-done | bytes 1048608 | tf_op jit(solution)/shard_map/while/body/eval_jaxpr/ppermute | solution.py:12
  141.0 17.2 %all-to-all-done = bf16[128,32,128]{2,0,1:T(8,128)(2,1)S(1)} async-done(((bf16[128,32,128]{2,0,1:T(8,128)(2,1)}), bf16[128,32,128]{2,0,1:T(8,128)(2,1)S(1)}, u32[]{:S(2)}, u32[]{:S(2)}) %all-to-all-start) | async-done | bytes 1048608 | tf_op jit(solution)/shard_map/while/body/eval_jaxpr/all_to_all | solution.py:52
  173.2 4.8 fusion.71
  206.2 15.2 %all-to-all-done.1 = bf16[32,1,128,1,128]{2,4,3,1,0:T(8,128)(2,1)} async-done(((bf16[32,1,128,1,128]{2,4,3,1,0:T(8,128)(2,1)}), bf16[32,1,128,1,128]{2,4,3,1,0:T(8,128)(2,1)}, u32[]{:S(2)}, u32[]{:S(2)}) %all-to-all-start.1) | async-done | bytes 1048608 | tf_op jit(solution)/shard_map/while/body/eval_jaxpr/all_to_all | solution.py:58
  228.3 25.0 %collective-permute-done = bf16[128,4096]{0,1:T(8,128)(2,1)S(1)} collective-permute-done((bf16[128,4096]{0,1:T(8,128)(2,1)}, bf16[128,4096]{0,1:T(8,128)(2,1)S(1)}, u32[]{:S(2)}, u32[]{:S(2)}) %collective-permute-start) | collective-permute-done | bytes 1048608 | tf_op jit(solution)/shard_map/while/body/eval_jaxpr/ppermute | solution.py:12
  261.8 17.2 %all-to-all-done = bf16[128,32,128]{2,0,1:T(8,128)(2,1)S(1)} async-done(((bf16[128,32,128]{2,0,1:T(8,128)(2,1)}), bf16[128,32,128]{2,0,1:T(8,128)(2,1)S(1)}, u32[]{:S(2)}, u32[]{:S(2)}) %all-to-all-start) | async-done | bytes 1048608 | tf_op jit(solution)/shard_map/while/body/eval_jaxpr/all_to_all | solution.py:52
  327.0 15.2 %all-to-all-done.1 = bf16[32,1,128,1,128]{2,4,3,1,0:T(8,128)(2,1)} async-done(((bf16[32,1,128,1,128]{2,4,3,1,0:T(8,128)(2,1)}), bf16[32,1,128,1,128]{2,4,3,1,0:T(8,128)(2,1)}, u32[]{:S(2)}, u32[]{:S(2)}) %all-to-all-start.1) | async-done | bytes 1048608 | tf_op jit(solution)/shard_map/while/body/eval_jaxpr/all_to_all | solution.py:58
  349.1 25.0 %collective-permute-done = bf16[128,4096]{0,1:T(8,128)(2,1)S(1)} collective-permute-done((bf16[128,4096]{0,1:T(8,128)(2,1)}, bf16[128,4096]{0,1:T(8,128)(2,1)S(1)}, u32[]{:S(2)}, u32[]{:S(2)}) %collective-permute-start) | collective-permute-done | bytes 1048608 | tf_op jit(solution)/shard_map/while/body/eval_jaxpr/ppermute | solution.py:12
  382.7 17.2 %all-to-all-done = bf16[128,32,128]{2,0,1:T(8,128)(2,1)S(1)} async-done(((bf16[128,32,128]{2,0,1:T(8,128)(2,1)}), bf16[128,32,128]{2,0,1:T(8,128)(2,1)S(1)}, u32[]{:S(2)}, u32[]{:S(2)}) %all-to-all-start) | async-done | bytes 1048608 | tf_op jit(solution)/shard_map/while/body/eval_jaxpr/all_to_all | solution.py:52
  447.9 15.2 %all-to-all-done.1 = bf16[32,1,128,1,128]{2,4,3,1,0:T(8,128)(2,1)} async-done(((bf16[32,1,128,1,128]{2,4,3,1,0:T(8,128)(2,1)}), bf16[32,1,128,1,128]{2,4,3,1,0:T(8,128)(2,1)}, u32[]{:S(2)}, u32[]{:S(2)}) %all-to-all-start.1) | async-done | bytes 1048608 | tf_op jit(solution)/shard_map/while/body/eval_jaxpr/all_to_all | solution.py:58
  470.0 25.0 %collective-permute-done = bf16[128,4096]{0,1:T(8,128)(2,1)S(1)} collective-permute-done((bf16[128,4096]{0,1:T(8,128)(2,1)}, bf16[128,4096]{0,1:T(8,128)(2,1)S(1)}, u32[]{:S(2)}, u32[]{:S(2)}) %collective-permute-start) | collective-permute-done | bytes 1048608 | tf_op jit(solution)/shard_map/while/body/eval_jaxpr/ppermute | solution.py:12
  503.5 17.2 %all-to-all-done = bf16[128,32,128]{2,0,1:T(8,128)(2,1)S(1)} async-done(((bf16[128,32,128]{2,0,1:T(8,128)(2,1)}), bf16[128,32,128]{2,0,1:T(8,128)(2,1)S(1)}, u32[]{:S(2)}, u32[]{:S(2)}) %all-to-all-start) | async-done | bytes 1048608 | tf_op jit(solution)/shard_map/while/body/eval_jaxpr/all_to_all | solution.py:52
  568.7 15.2 %all-to-all-done.1 = bf16[32,1,128,1,128]{2,4,3,1,0:T(8,128)(2,1)} async-done(((bf16[32,1,128,1,128]{2,4,3,1,0:T(8,128)(2,1)}), bf16[32,1,128,1,128]{2,4,3,1,0:T(8,128)(2,1)}, u32[]{:S(2)}, u32[]{:S(2)}) %all-to-all-start.1) | async-done | bytes 1048608 | tf_op jit(solution)/shard_map/while/body/eval_jaxpr/all_to_all | solution.py:58
  590.8 25.0 %collective-permute-done = bf16[128,4096]{0,1:T(8,128)(2,1)S(1)} collective-permute-done((bf16[128,4096]{0,1:T(8,128)(2,1)}, bf16[128,4096]{0,1:T(8,128)(2,1)S(1)}, u32[]{:S(2)}, u32[]{:S(2)}) %collective-permute-start) | collective-permute-done | bytes 1048608 | tf_op jit(solution)/shard_map/while/body/eval_jaxpr/ppermute | solution.py:12
  624.4 17.2 %all-to-all-done = bf16[128,32,128]{2,0,1:T(8,128)(2,1)S(1)} async-done(((bf16[128,32,128]{2,0,1:T(8,128)(2,1)}), bf16[128,32,128]{2,0,1:T(8,128)(2,1)S(1)}, u32[]{:S(2)}, u32[]{:S(2)}) %all-to-all-start) | async-done | bytes 1048608 | tf_op jit(solution)/shard_map/while/body/eval_jaxpr/all_to_all | solution.py:52
  689.6 15.2 %all-to-all-done.1 = bf16[32,1,128,1,128]{2,4,3,1,0:T(8,128)(2,1)} async-done(((bf16[32,1,128,1,128]{2,4,3,1,0:T(8,128)(2,1)}), bf16[32,1,128,1,128]{2,4,3,1,0:T(8,128)(2,1)}, u32[]{:S(2)}, u32[]{:S(2)}) %all-to-all-start.1) | async-done | bytes 1048608 | tf_op jit(solution)/shard_map/while/body/eval_jaxpr/all_to_all | solution.py:58
  711.7 25.0 %collective-permute-done = bf16[128,4096]{0,1:T(8,128)(2,1)S(1)} collective-permute-done((bf16[128,4096]{0,1:T(8,128)(2,1)}, bf16[128,4096]{0,1:T(8,128)(2,1)S(1)}, u32[]{:S(2)}, u32[]{:S(2)}) %collective-permute-start) | collective-permute-done | bytes 1048608 | tf_op jit(solution)/shard_map/while/body/eval_jaxpr/ppermute | solution.py:12
  745.2 17.2 %all-to-all-done = bf16[128,32,128]{2,0,1:T(8,128)(2,1)S(1)} async-done(((bf16[128,32,128]{2,0,1:T(8,128)(2,1)}), bf16[128,32,128]{2,0,1:T(8,128)(2,1)S(1)}, u32[]{:S(2)}, u32[]{:S(2)}) %all-to-all-start) | async-done | bytes 1048608 | tf_op jit(solution)/shard_map/while/body/eval_jaxpr/all_to_all | solution.py:52
  810.4 15.2 %all-to-all-done.1 = bf16[32,1,128,1,128]{2,4,3,1,0:T(8,128)(2,1)} async-done(((bf16[32,1,128,1,128]{2,4,3,1,0:T(8,128)(2,1)}), bf16[32,1,128,1,128]{2,4,3,1,0:T(8,128)(2,1)}, u32[]{:S(2)}, u32[]{:S(2)}) %all-to-all-start.1) | async-done | bytes 1048608 | tf_op jit(solution)/shard_map/while/body/eval_jaxpr/all_to_all | solution.py:58
  832.5 25.0 %collective-permute-done = bf16[128,4096]{0,1:T(8,128)(2,1)S(1)} collective-permute-done((bf16[128,4096]{0,1:T(8,128)(2,1)}, bf16[128,4096]{0,1:T(8,128)(2,1)S(1)}, u32[]{:S(2)}, u32[]{:S(2)}) %collective-permute-start) | collective-permute-done | bytes 1048608 | tf_op jit(solution)/shard_map/while/body/eval_jaxpr/ppermute | solution.py:12
  866.1 17.2 %all-to-all-done = bf16[128,32,128]{2,0,1:T(8,128)(2,1)S(1)} async-done(((bf16[128,32,128]{2,0,1:T(8,128)(2,1)}), bf16[128,32,128]{2,0,1:T(8,128)(2,1)S(1)}, u32[]{:S(2)}, u32[]{:S(2)}) %all-to-all-start) | async-done | bytes 1048608 | tf_op jit(solution)/shard_map/while/body/eval_jaxpr/all_to_all | solution.py:52
  931.3 15.2 %all-to-all-done.1 = bf16[32,1,128,1,128]{2,4,3,1,0:T(8,128)(2,1)} async-done(((bf16[32,1,128,1,128]{2,4,3,1,0:T(8,128)(2,1)}), bf16[32,1,128,1,128]{2,4,3,1,0:T(8,128)(2,1)}, u32[]{:S(2)}, u32[]{:S(2)}) %all-to-all-start.1) | async-done | bytes 1048608 | tf_op jit(solution)/shard_map/while/body/eval_jaxpr/all_to_all | solution.py:58
  953.4 25.0 %collective-permute-done = bf16[128,4096]{0,1:T(8,128)(2,1)S(1)} collective-permute-done((bf16[128,4096]{0,1:T(8,128)(2,1)}, bf16[128,4096]{0,1:T(8,128)(2,1)S(1)}, u32[]{:S(2)}, u32[]{:S(2)}) %collective-permute-start) | collective-permute-done | bytes 1048608 | tf_op jit(solution)/shard_map/while/body/eval_jaxpr/ppermute | solution.py:12
  986.9 17.2 %all-to-all-done = bf16[128,32,128]{2,0,1:T(8,128)(2,1)S(1)} async-done(((bf16[128,32,128]{2,0,1:T(8,128)(2,1)}), bf16[128,32,128]{2,0,1:T(8,128)(2,1)S(1)}, u32[]{:S(2)}, u32[]{:S(2)}) %all-to-all-start) | async-done | bytes 1048608 | tf_op jit(solution)/shard_map/while/body/eval_jaxpr/all_to_all | solution.py:52
  1052.1 15.2 %all-to-all-done.1 = bf16[32,1,128,1,128]{2,4,3,1,0:T(8,128)(2,1)} async-done(((bf16[32,1,128,1,128]{2,4,3,1,0:T(8,128)(2,1)}), bf16[32,1,128,1,128]{2,4,3,1,0:T(8,128)(2,1)}, u32[]{:S(2)}, u32[]{:S(2)}) %all-to-all-start.1) | async-done | bytes 1048608 | tf_op jit(solution)/shard_map/while/body/eval_jaxpr/all_to_all | solution.py:58
  1074.2 25.0 %collective-permute-done = bf16[128,4096]{0,1:T(8,128)(2,1)S(1)} collective-permute-done((bf16[128,4096]{0,1:T(8,128)(2,1)}, bf16[128,4096]{0,1:T(8,128)(2,1)S(1)}, u32[]{:S(2)}, u32[]{:S(2)}) %collective-permute-start) | collective-permute-done | bytes 1048608 | tf_op jit(solution)/shard_map/while/body/eval_jaxpr/ppermute | solution.py:12
  (568 shorter events, 559.1 us)
Async XLA Ops:
  6.5 1.7 copy-start
  12.8 24.5 %all-to-all-start = ((bf16[128,32,128]{2,0,1:T(8,128)(2,1)}), bf16[128,32,128]{2,0,1:T(8,128)(2,1)S(1)}, u32[]{:S(2)}, u32[]{:S(2)}) async-start(bf16[128,32,128]{2,0,1:T(8,128)(2,1)} %copy.92), calls=%async_computation | async-start | bytes 2097152 | tf_op jit(solution)/shard_map/while/body/eval_jaxpr/all_to_all | solution.py:52
  78.7 21.9 %all-to-all-start.1 = ((bf16[32,1,128,1,128]{2,4,3,1,0:T(8,128)(2,1)}), bf16[32,1,128,1,128]{2,4,3,1,0:T(8,128)(2,1)}, u32[]{:S(2)}, u32[]{:S(2)}) async-start(bf16[32,1,128,1,128]{2,4,3,1,0:T(8,128)(2,1)} %constant_dynamic-update-slice_fusion.97), calls=%async_computation.1 | async-start | bytes 2097152 | tf_op jit(solution)/shard_map/while/body/eval_jaxpr/all_to_all | solution.py:58
  103.9 28.5 %collective-permute-start = (bf16[128,4096]{0,1:T(8,128)(2,1)}, bf16[128,4096]{0,1:T(8,128)(2,1)S(1)}, u32[]{:S(2)}, u32[]{:S(2)}) collective-permute-start(bf16[128,4096]{0,1:T(8,128)(2,1)} %get-tuple-element.264), channel_id=1, source_target_pairs={{0,32},{32,64},{64,96},{96,128},{128,160},{160,192},{192,224},{1,3... | collective-permute-start | bytes 3145736 | tf_op jit(solution)/shard_map/while/body/eval_jaxpr/ppermute | solution.py:12
  137.0 21.1 %all-to-all-start = ((bf16[128,32,128]{2,0,1:T(8,128)(2,1)}), bf16[128,32,128]{2,0,1:T(8,128)(2,1)S(1)}, u32[]{:S(2)}, u32[]{:S(2)}) async-start(bf16[128,32,128]{2,0,1:T(8,128)(2,1)} %copy.92), calls=%async_computation | async-start | bytes 2097152 | tf_op jit(solution)/shard_map/while/body/eval_jaxpr/all_to_all | solution.py:52
  199.5 21.9 %all-to-all-start.1 = ((bf16[32,1,128,1,128]{2,4,3,1,0:T(8,128)(2,1)}), bf16[32,1,128,1,128]{2,4,3,1,0:T(8,128)(2,1)}, u32[]{:S(2)}, u32[]{:S(2)}) async-start(bf16[32,1,128,1,128]{2,4,3,1,0:T(8,128)(2,1)} %constant_dynamic-update-slice_fusion.97), calls=%async_computation.1 | async-start | bytes 2097152 | tf_op jit(solution)/shard_map/while/body/eval_jaxpr/all_to_all | solution.py:58
  224.8 28.5 %collective-permute-start = (bf16[128,4096]{0,1:T(8,128)(2,1)}, bf16[128,4096]{0,1:T(8,128)(2,1)S(1)}, u32[]{:S(2)}, u32[]{:S(2)}) collective-permute-start(bf16[128,4096]{0,1:T(8,128)(2,1)} %get-tuple-element.264), channel_id=1, source_target_pairs={{0,32},{32,64},{64,96},{96,128},{128,160},{160,192},{192,224},{1,3... | collective-permute-start | bytes 3145736 | tf_op jit(solution)/shard_map/while/body/eval_jaxpr/ppermute | solution.py:12
  257.9 21.1 %all-to-all-start = ((bf16[128,32,128]{2,0,1:T(8,128)(2,1)}), bf16[128,32,128]{2,0,1:T(8,128)(2,1)S(1)}, u32[]{:S(2)}, u32[]{:S(2)}) async-start(bf16[128,32,128]{2,0,1:T(8,128)(2,1)} %copy.92), calls=%async_computation | async-start | bytes 2097152 | tf_op jit(solution)/shard_map/while/body/eval_jaxpr/all_to_all | solution.py:52
  320.4 21.9 %all-to-all-start.1 = ((bf16[32,1,128,1,128]{2,4,3,1,0:T(8,128)(2,1)}), bf16[32,1,128,1,128]{2,4,3,1,0:T(8,128)(2,1)}, u32[]{:S(2)}, u32[]{:S(2)}) async-start(bf16[32,1,128,1,128]{2,4,3,1,0:T(8,128)(2,1)} %constant_dynamic-update-slice_fusion.97), calls=%async_computation.1 | async-start | bytes 2097152 | tf_op jit(solution)/shard_map/while/body/eval_jaxpr/all_to_all | solution.py:58
  345.6 28.5 %collective-permute-start = (bf16[128,4096]{0,1:T(8,128)(2,1)}, bf16[128,4096]{0,1:T(8,128)(2,1)S(1)}, u32[]{:S(2)}, u32[]{:S(2)}) collective-permute-start(bf16[128,4096]{0,1:T(8,128)(2,1)} %get-tuple-element.264), channel_id=1, source_target_pairs={{0,32},{32,64},{64,96},{96,128},{128,160},{160,192},{192,224},{1,3... | collective-permute-start | bytes 3145736 | tf_op jit(solution)/shard_map/while/body/eval_jaxpr/ppermute | solution.py:12
  378.7 21.1 %all-to-all-start = ((bf16[128,32,128]{2,0,1:T(8,128)(2,1)}), bf16[128,32,128]{2,0,1:T(8,128)(2,1)S(1)}, u32[]{:S(2)}, u32[]{:S(2)}) async-start(bf16[128,32,128]{2,0,1:T(8,128)(2,1)} %copy.92), calls=%async_computation | async-start | bytes 2097152 | tf_op jit(solution)/shard_map/while/body/eval_jaxpr/all_to_all | solution.py:52
  441.2 21.9 %all-to-all-start.1 = ((bf16[32,1,128,1,128]{2,4,3,1,0:T(8,128)(2,1)}), bf16[32,1,128,1,128]{2,4,3,1,0:T(8,128)(2,1)}, u32[]{:S(2)}, u32[]{:S(2)}) async-start(bf16[32,1,128,1,128]{2,4,3,1,0:T(8,128)(2,1)} %constant_dynamic-update-slice_fusion.97), calls=%async_computation.1 | async-start | bytes 2097152 | tf_op jit(solution)/shard_map/while/body/eval_jaxpr/all_to_all | solution.py:58
  466.5 28.5 %collective-permute-start = (bf16[128,4096]{0,1:T(8,128)(2,1)}, bf16[128,4096]{0,1:T(8,128)(2,1)S(1)}, u32[]{:S(2)}, u32[]{:S(2)}) collective-permute-start(bf16[128,4096]{0,1:T(8,128)(2,1)} %get-tuple-element.264), channel_id=1, source_target_pairs={{0,32},{32,64},{64,96},{96,128},{128,160},{160,192},{192,224},{1,3... | collective-permute-start | bytes 3145736 | tf_op jit(solution)/shard_map/while/body/eval_jaxpr/ppermute | solution.py:12
  499.6 21.1 %all-to-all-start = ((bf16[128,32,128]{2,0,1:T(8,128)(2,1)}), bf16[128,32,128]{2,0,1:T(8,128)(2,1)S(1)}, u32[]{:S(2)}, u32[]{:S(2)}) async-start(bf16[128,32,128]{2,0,1:T(8,128)(2,1)} %copy.92), calls=%async_computation | async-start | bytes 2097152 | tf_op jit(solution)/shard_map/while/body/eval_jaxpr/all_to_all | solution.py:52
  562.1 21.9 %all-to-all-start.1 = ((bf16[32,1,128,1,128]{2,4,3,1,0:T(8,128)(2,1)}), bf16[32,1,128,1,128]{2,4,3,1,0:T(8,128)(2,1)}, u32[]{:S(2)}, u32[]{:S(2)}) async-start(bf16[32,1,128,1,128]{2,4,3,1,0:T(8,128)(2,1)} %constant_dynamic-update-slice_fusion.97), calls=%async_computation.1 | async-start | bytes 2097152 | tf_op jit(solution)/shard_map/while/body/eval_jaxpr/all_to_all | solution.py:58
  587.3 28.5 %collective-permute-start = (bf16[128,4096]{0,1:T(8,128)(2,1)}, bf16[128,4096]{0,1:T(8,128)(2,1)S(1)}, u32[]{:S(2)}, u32[]{:S(2)}) collective-permute-start(bf16[128,4096]{0,1:T(8,128)(2,1)} %get-tuple-element.264), channel_id=1, source_target_pairs={{0,32},{32,64},{64,96},{96,128},{128,160},{160,192},{192,224},{1,3... | collective-permute-start | bytes 3145736 | tf_op jit(solution)/shard_map/while/body/eval_jaxpr/ppermute | solution.py:12
  620.4 21.1 %all-to-all-start = ((bf16[128,32,128]{2,0,1:T(8,128)(2,1)}), bf16[128,32,128]{2,0,1:T(8,128)(2,1)S(1)}, u32[]{:S(2)}, u32[]{:S(2)}) async-start(bf16[128,32,128]{2,0,1:T(8,128)(2,1)} %copy.92), calls=%async_computation | async-start | bytes 2097152 | tf_op jit(solution)/shard_map/while/body/eval_jaxpr/all_to_all | solution.py:52
  682.9 21.9 %all-to-all-start.1 = ((bf16[32,1,128,1,128]{2,4,3,1,0:T(8,128)(2,1)}), bf16[32,1,128,1,128]{2,4,3,1,0:T(8,128)(2,1)}, u32[]{:S(2)}, u32[]{:S(2)}) async-start(bf16[32,1,128,1,128]{2,4,3,1,0:T(8,128)(2,1)} %constant_dynamic-update-slice_fusion.97), calls=%async_computation.1 | async-start | bytes 2097152 | tf_op jit(solution)/shard_map/while/body/eval_jaxpr/all_to_all | solution.py:58
  708.2 28.5 %collective-permute-start = (bf16[128,4096]{0,1:T(8,128)(2,1)}, bf16[128,4096]{0,1:T(8,128)(2,1)S(1)}, u32[]{:S(2)}, u32[]{:S(2)}) collective-permute-start(bf16[128,4096]{0,1:T(8,128)(2,1)} %get-tuple-element.264), channel_id=1, source_target_pairs={{0,32},{32,64},{64,96},{96,128},{128,160},{160,192},{192,224},{1,3... | collective-permute-start | bytes 3145736 | tf_op jit(solution)/shard_map/while/body/eval_jaxpr/ppermute | solution.py:12
  741.3 21.1 %all-to-all-start = ((bf16[128,32,128]{2,0,1:T(8,128)(2,1)}), bf16[128,32,128]{2,0,1:T(8,128)(2,1)S(1)}, u32[]{:S(2)}, u32[]{:S(2)}) async-start(bf16[128,32,128]{2,0,1:T(8,128)(2,1)} %copy.92), calls=%async_computation | async-start | bytes 2097152 | tf_op jit(solution)/shard_map/while/body/eval_jaxpr/all_to_all | solution.py:52
  803.8 21.9 %all-to-all-start.1 = ((bf16[32,1,128,1,128]{2,4,3,1,0:T(8,128)(2,1)}), bf16[32,1,128,1,128]{2,4,3,1,0:T(8,128)(2,1)}, u32[]{:S(2)}, u32[]{:S(2)}) async-start(bf16[32,1,128,1,128]{2,4,3,1,0:T(8,128)(2,1)} %constant_dynamic-update-slice_fusion.97), calls=%async_computation.1 | async-start | bytes 2097152 | tf_op jit(solution)/shard_map/while/body/eval_jaxpr/all_to_all | solution.py:58
  829.0 28.5 %collective-permute-start = (bf16[128,4096]{0,1:T(8,128)(2,1)}, bf16[128,4096]{0,1:T(8,128)(2,1)S(1)}, u32[]{:S(2)}, u32[]{:S(2)}) collective-permute-start(bf16[128,4096]{0,1:T(8,128)(2,1)} %get-tuple-element.264), channel_id=1, source_target_pairs={{0,32},{32,64},{64,96},{96,128},{128,160},{160,192},{192,224},{1,3... | collective-permute-start | bytes 3145736 | tf_op jit(solution)/shard_map/while/body/eval_jaxpr/ppermute | solution.py:12
  862.1 21.1 %all-to-all-start = ((bf16[128,32,128]{2,0,1:T(8,128)(2,1)}), bf16[128,32,128]{2,0,1:T(8,128)(2,1)S(1)}, u32[]{:S(2)}, u32[]{:S(2)}) async-start(bf16[128,32,128]{2,0,1:T(8,128)(2,1)} %copy.92), calls=%async_computation | async-start | bytes 2097152 | tf_op jit(solution)/shard_map/while/body/eval_jaxpr/all_to_all | solution.py:52
  924.6 21.9 %all-to-all-start.1 = ((bf16[32,1,128,1,128]{2,4,3,1,0:T(8,128)(2,1)}), bf16[32,1,128,1,128]{2,4,3,1,0:T(8,128)(2,1)}, u32[]{:S(2)}, u32[]{:S(2)}) async-start(bf16[32,1,128,1,128]{2,4,3,1,0:T(8,128)(2,1)} %constant_dynamic-update-slice_fusion.97), calls=%async_computation.1 | async-start | bytes 2097152 | tf_op jit(solution)/shard_map/while/body/eval_jaxpr/all_to_all | solution.py:58
  949.9 28.5 %collective-permute-start = (bf16[128,4096]{0,1:T(8,128)(2,1)}, bf16[128,4096]{0,1:T(8,128)(2,1)S(1)}, u32[]{:S(2)}, u32[]{:S(2)}) collective-permute-start(bf16[128,4096]{0,1:T(8,128)(2,1)} %get-tuple-element.264), channel_id=1, source_target_pairs={{0,32},{32,64},{64,96},{96,128},{128,160},{160,192},{192,224},{1,3... | collective-permute-start | bytes 3145736 | tf_op jit(solution)/shard_map/while/body/eval_jaxpr/ppermute | solution.py:12
  983.0 21.1 %all-to-all-start = ((bf16[128,32,128]{2,0,1:T(8,128)(2,1)}), bf16[128,32,128]{2,0,1:T(8,128)(2,1)S(1)}, u32[]{:S(2)}, u32[]{:S(2)}) async-start(bf16[128,32,128]{2,0,1:T(8,128)(2,1)} %copy.92), calls=%async_computation | async-start | bytes 2097152 | tf_op jit(solution)/shard_map/while/body/eval_jaxpr/all_to_all | solution.py:52
  1045.5 21.9 %all-to-all-start.1 = ((bf16[32,1,128,1,128]{2,4,3,1,0:T(8,128)(2,1)}), bf16[32,1,128,1,128]{2,4,3,1,0:T(8,128)(2,1)}, u32[]{:S(2)}, u32[]{:S(2)}) async-start(bf16[32,1,128,1,128]{2,4,3,1,0:T(8,128)(2,1)} %constant_dynamic-update-slice_fusion.97), calls=%async_computation.1 | async-start | bytes 2097152 | tf_op jit(solution)/shard_map/while/body/eval_jaxpr/all_to_all | solution.py:58
  1070.7 28.5 %collective-permute-start = (bf16[128,4096]{0,1:T(8,128)(2,1)}, bf16[128,4096]{0,1:T(8,128)(2,1)S(1)}, u32[]{:S(2)}, u32[]{:S(2)}) collective-permute-start(bf16[128,4096]{0,1:T(8,128)(2,1)} %get-tuple-element.264), channel_id=1, source_target_pairs={{0,32},{32,64},{64,96},{96,128},{128,160},{160,192},{192,224},{1,3... | collective-permute-start | bytes 3145736 | tf_op jit(solution)/shard_map/while/body/eval_jaxpr/ppermute | solution.py:12
